TPU v7x, 32 devices: a whole 2x2x4 slice. The times are simulated.
32 devices in a mesh: batch: 8 (over z, y), tensor: 4 (over x, core).
Axes of the slice: x: 2, y: 2, z: 4, core: 2. Of those that a mesh axis runs over, the one named last changes fastest.
Arguments:
- tokens: bfloat16 [12288, 768], P('batch'), may hold values from -6 to 6
- lengths: int32 [8], P('batch'), may hold values from 1024 to 1536, as said below
- w_query: bfloat16 [768, 768], P('batch', 'tensor'), may hold values from -0.4375 to 0.4375
- w_key: bfloat16 [768, 768], P('batch', 'tensor'), may hold values from -0.21875 to 0.21875
- w_value: bfloat16 [768, 768], P('batch', 'tensor'), may hold values from -0.21875 to 0.21875
- w_out: bfloat16 [768, 768], P('tensor', 'batch'), may hold values from -0.875 to 0.875
- w_up: bfloat16 [768, 3072], P('batch', 'tensor'), may hold values from -0.21875 to 0.21875
- w_down: bfloat16 [3072, 768], P('tensor', 'batch'), may hold values from -0.109375 to 0.109375
- norm_gain: bfloat16 [2, 768], P(None, 'batch'), may hold values from 0.099609375 to 1.8984375
- norm_shift: bfloat16 [2, 768], P(None, 'batch'), may hold values from -3 to 3
- out_grad: bfloat16 [12288, 768], P('batch'), may hold values from -6 to 6
Outputs:
- layer_out: bfloat16 [12288, 768], P('batch')
- grad_input: bfloat16 [12288, 768], P('batch')
- grad_query: float32 [768, 768], P('batch', 'tensor')
- grad_key: float32 [768, 768], P('batch', 'tensor')
- grad_value: float32 [768, 768], P('batch', 'tensor')
- grad_out: float32 [768, 768], P('tensor', 'batch')
- grad_up: float32 [768, 3072], P('batch', 'tensor')
- grad_down: float32 [3072, 768], P('tensor', 'batch')
- grad_gain: float32 [2, 768], P(None, 'batch')
- grad_shift: float32 [2, 768], P(None, 'batch')
Inputs may be any that keep to these rules, and one draw needn't show every extreme that they name: `lengths`: each sequence's valid tokens; some sequence fills all 1536 slots.
All inputs are finite; a program needn't handle non-finite values.
Results may differ from a plain program's by a relative error of at most 0.017.
Values may be sent and summed in bfloat16 or wider, within the bound.
No kernel may reach another device: no remote copies, remote signals or barrier semaphores. Data moves between devices by JAX's collectives and lax.ppermute only.
A program may use at most 192 MiB of HBM per device.

v0:
```python
import jax
import jax.numpy as jnp
from jax import lax
from jax.sharding import PartitionSpec as P

HD = 64
epsilon = 1e-05


def cut_along(value, dim, length):
    shape = value.shape
    parts = value.reshape(*shape[:dim], length, shape[dim] // length, *shape[dim + 1 :])
    return jnp.moveaxis(parts, dim, 0)


def summed_on_arrival(value, axis, dim):
    length = lax.axis_size(axis)
    parts = lax.all_to_all(cut_along(value, dim, length), axis, 0, 0, tiled=True)
    return jnp.sum(parts.astype(jnp.float32), axis=0)


def normalize_keep(values, gain_row, shift_row):
    middle = jnp.mean(values, axis=-1, keepdims=True)
    centred = values - middle
    spread = jnp.mean(centred * centred, axis=-1, keepdims=True)
    inverse = lax.rsqrt(spread + epsilon)
    scaled = centred * inverse
    return (scaled * gain_row + shift_row, scaled, inverse)


def normalize_back(grad_normed, scaled, inverse, gain_row):
    grad_scaled = grad_normed * gain_row
    mean_grad = jnp.mean(grad_scaled, axis=-1, keepdims=True)
    mean_cross = jnp.mean(grad_scaled * scaled, axis=-1, keepdims=True)
    grad_values = inverse * (grad_scaled - mean_grad - scaled * mean_cross)
    return (grad_values, jnp.sum(grad_normed * scaled, axis=0), jnp.sum(grad_normed, axis=0))


def multiply(left_mat, right_mat):
    return jnp.dot(left_mat, right_mat, preferred_element_type=jnp.float32)


def inner_rows(left_mat, right_mat):
    return lax.dot_general(
        left_mat, right_mat, (((0,), (0,)), ((), ())), preferred_element_type=jnp.float32
    )


def outer_cols(left_mat, right_mat):
    return lax.dot_general(
        left_mat, right_mat, (((1,), (1,)), ((), ())), preferred_element_type=jnp.float32
    )


def gelu_tanh(values):
    return jax.nn.gelu(values, approximate=True)


def score_block(queries_blk, keys_part, row_pos, key_pos, length, scaling):
    raw_scores = jnp.einsum(
        "qhd,khd->hqk", queries_blk, keys_part, preferred_element_type=jnp.float32
    )
    scores = raw_scores * scaling
    allowed = (key_pos[None, :] <= row_pos[:, None]) & (key_pos[None, :] < length)
    magnitude = jnp.where(allowed[None], jnp.abs(scores), -1e30)
    return (scores, magnitude)


def attend_forward(queries, key_rows, value_rows, length, block_rows, scaling):
    seq_rows = queries.shape[0]
    position = jnp.arange(seq_rows, dtype=jnp.int32)
    outputs = []
    log_sums = []
    for number in range(seq_rows // block_rows):
        begin_row = number * block_rows
        end_row = begin_row + block_rows
        scores, magnitude = score_block(
            queries[begin_row:end_row],
            key_rows[:end_row],
            position[begin_row:end_row],
            position[:end_row],
            length,
            scaling,
        )
        row_max = jnp.max(magnitude, axis=-1, keepdims=True)
        exponent = jnp.exp(magnitude - row_max)
        row_sum = jnp.sum(exponent, axis=-1, keepdims=True)
        weights = (jnp.sign(scores) * (exponent / row_sum)).astype(jnp.bfloat16)
        outputs.append(
            jnp.einsum(
                "hqk,khd->qhd", weights, value_rows[:end_row], preferred_element_type=jnp.float32
            )
        )
        log_sums.append(row_max + jnp.log(row_sum))
    return (jnp.concatenate(outputs, axis=0), jnp.concatenate(log_sums, axis=1))


def attend_back(queries, key_rows, value_rows, grad_mixed, log_sums, length, block_rows, scaling):
    seq_rows = queries.shape[0]
    position = jnp.arange(seq_rows, dtype=jnp.int32)
    grad_queries = []
    grad_keys = jnp.zeros(key_rows.shape, jnp.float32)
    grad_values = jnp.zeros(value_rows.shape, jnp.float32)
    for number in range(seq_rows // block_rows):
        begin_row = number * block_rows
        end_row = begin_row + block_rows
        scores, magnitude = score_block(
            queries[begin_row:end_row],
            key_rows[:end_row],
            position[begin_row:end_row],
            position[:end_row],
            length,
            scaling,
        )
        probability = jnp.exp(magnitude - log_sums[:, begin_row:end_row])
        signs = jnp.sign(scores)
        weights = signs * probability
        grad_blk = grad_mixed[begin_row:end_row]
        grad_weights = jnp.einsum(
            "qhd,khd->hqk", grad_blk, value_rows[:end_row], preferred_element_type=jnp.float32
        )
        delta_row = jnp.sum(weights * grad_weights, axis=-1, keepdims=True)
        grad_raw = (signs * probability * (signs * grad_weights - delta_row) * scaling).astype(
            jnp.bfloat16
        )
        grad_queries.append(
            jnp.einsum(
                "hqk,khd->qhd", grad_raw, key_rows[:end_row], preferred_element_type=jnp.float32
            )
        )
        grad_keys = grad_keys.at[:end_row].add(
            jnp.einsum(
                "hqk,qhd->khd",
                grad_raw,
                queries[begin_row:end_row],
                preferred_element_type=jnp.float32,
            )
        )
        grad_values = grad_values.at[:end_row].add(
            jnp.einsum(
                "hqk,qhd->khd",
                weights.astype(jnp.bfloat16),
                grad_blk,
                preferred_element_type=jnp.float32,
            )
        )
    return (jnp.concatenate(grad_queries, axis=0), grad_keys, grad_values)


def per_device(
    tokens, lengths, w_query, w_key, w_value, w_out, w_up, w_down, norm_gain, norm_shift, out_grad
):
    seq_rows = tokens.shape[0]
    seq_count = lengths.shape[0]
    seq_len = seq_rows // seq_count
    position = jnp.arange(seq_rows, dtype=jnp.int32)
    slot_length = jnp.repeat(lengths, seq_len)
    is_valid = (position % seq_len < slot_length).astype(jnp.float32)[:, None]
    block_rows = min(512, seq_len)
    scaling = float(HD) ** (-0.5)
    gathered = (
        lax.all_gather(w_query, "batch", axis=0, tiled=True),
        lax.all_gather(w_key, "batch", axis=0, tiled=True),
        lax.all_gather(w_value, "batch", axis=0, tiled=True),
        lax.all_gather(w_out, "batch", axis=1, tiled=True),
        lax.all_gather(w_up, "batch", axis=0, tiled=True),
        lax.all_gather(w_down, "batch", axis=1, tiled=True),
        lax.all_gather(norm_gain, "batch", axis=1, tiled=True),
        lax.all_gather(norm_shift, "batch", axis=1, tiled=True),
    )
    full_query, full_key, full_value, full_out, full_up, full_down, gain_full, shift_full = gathered
    gain_rows = gain_full.astype(jnp.float32)
    shift_rows = shift_full.astype(jnp.float32)
    head_count = full_query.shape[1] // HD

    def per_sequence(values):
        return values.reshape(seq_count, seq_len, head_count, HD)

    inputs = tokens.astype(jnp.float32)
    normed, scaled_one, inverse_one = normalize_keep(inputs, gain_rows[0], shift_rows[0])
    normed_low = normed.astype(jnp.bfloat16)
    queries = (
        multiply(normed_low, full_query).astype(jnp.bfloat16).reshape(seq_rows, head_count, HD)
    )
    key_rows = multiply(normed_low, full_key).astype(jnp.bfloat16).reshape(seq_rows, head_count, HD)
    value_rows = (
        multiply(normed_low, full_value).astype(jnp.bfloat16).reshape(seq_rows, head_count, HD)
    )

    def forward_one(items):
        return attend_forward(items[0], items[1], items[2], items[3], block_rows, scaling)

    mixed_heads, log_sums = lax.map(
        forward_one,
        (per_sequence(queries), per_sequence(key_rows), per_sequence(value_rows), lengths),
    )
    mixed_low = mixed_heads.reshape(seq_rows, head_count * HD).astype(jnp.bfloat16)
    attn_partial = multiply(mixed_low, full_out)
    hidden = inputs + lax.psum(attn_partial, "tensor")
    normed_two, scaled_two, inverse_two = normalize_keep(hidden, gain_rows[1], shift_rows[1])
    normed_two_low = normed_two.astype(jnp.bfloat16)
    up_proj = multiply(normed_two_low, full_up)
    active_full, gelu_pull = jax.vjp(gelu_tanh, up_proj)
    active = active_full.astype(jnp.bfloat16)
    down_partial = multiply(active, full_down)
    branch = lax.psum(down_partial.astype(jnp.bfloat16), "tensor").astype(jnp.float32)
    out_rows = ((hidden + branch) * is_valid).astype(jnp.bfloat16)
    grad_rows = out_grad * is_valid.astype(jnp.bfloat16)
    grad_down = inner_rows(active, grad_rows)
    grad_active = outer_cols(grad_rows, full_down)
    grad_upper = gelu_pull(grad_active)[0].astype(jnp.bfloat16)
    grad_up = inner_rows(normed_two_low, grad_upper)
    mid_partial = outer_cols(grad_upper, full_up)
    grad_normed_two = lax.psum(mid_partial, "tensor")
    grad_from_two, gain_two, shift_two = normalize_back(
        grad_normed_two, scaled_two, inverse_two, gain_rows[1]
    )
    grad_hidden = grad_rows.astype(jnp.float32) + grad_from_two
    grad_attn = grad_hidden.astype(jnp.bfloat16)
    grad_out = inner_rows(mixed_low, grad_attn)
    grad_mixed = (
        outer_cols(grad_attn, full_out).astype(jnp.bfloat16).reshape(seq_rows, head_count, HD)
    )

    def backward_one(items):
        return attend_back(
            items[0], items[1], items[2], items[3], items[4], items[5], block_rows, scaling
        )

    grad_queries, grad_keys, grad_values = lax.map(
        backward_one,
        (
            per_sequence(queries),
            per_sequence(key_rows),
            per_sequence(value_rows),
            per_sequence(grad_mixed),
            log_sums,
            lengths,
        ),
    )
    queries_low = grad_queries.astype(jnp.bfloat16).reshape(seq_rows, head_count * HD)
    keys_low = grad_keys.astype(jnp.bfloat16).reshape(seq_rows, head_count * HD)
    values_low = grad_values.astype(jnp.bfloat16).reshape(seq_rows, head_count * HD)
    grad_query = inner_rows(normed_low, queries_low)
    grad_key = inner_rows(normed_low, keys_low)
    grad_value = inner_rows(normed_low, values_low)
    partial_in = (
        outer_cols(queries_low, full_query)
        + outer_cols(keys_low, full_key)
        + outer_cols(values_low, full_value)
    )
    grad_normed = lax.psum(partial_in.astype(jnp.bfloat16), "tensor").astype(jnp.float32)
    grad_from_one, gain_one, shift_one = normalize_back(
        grad_normed, scaled_one, inverse_one, gain_rows[0]
    )
    grad_input = (grad_hidden + grad_from_one).astype(jnp.bfloat16)
    gain_pair = jnp.stack([gain_one, gain_two])
    shift_pair = jnp.stack([shift_one, shift_two])
    everything = (
        summed_on_arrival(grad_query.astype(jnp.bfloat16), "batch", 0),
        summed_on_arrival(grad_key.astype(jnp.bfloat16), "batch", 0),
        summed_on_arrival(grad_value.astype(jnp.bfloat16), "batch", 0),
        summed_on_arrival(grad_out.astype(jnp.bfloat16), "batch", 1),
        summed_on_arrival(grad_up.astype(jnp.bfloat16), "batch", 0),
        summed_on_arrival(grad_down.astype(jnp.bfloat16), "batch", 1),
        summed_on_arrival(gain_pair.astype(jnp.bfloat16), "batch", 1),
        summed_on_arrival(shift_pair.astype(jnp.bfloat16), "batch", 1),
    )
    (
        shard_query,
        shard_key,
        shard_value,
        shard_out,
        shard_up,
        shard_down,
        shard_gain,
        shard_shift,
    ) = everything
    return (
        out_rows,
        grad_input,
        shard_query,
        shard_key,
        shard_value,
        shard_out,
        shard_up,
        shard_down,
        shard_gain,
        shard_shift,
    )


def solution(mesh):
    in_specs = (
        P("batch", None),
        P("batch"),
        P("batch", "tensor"),
        P("batch", "tensor"),
        P("batch", "tensor"),
        P("tensor", "batch"),
        P("batch", "tensor"),
        P("tensor", "batch"),
        P(None, "batch"),
        P(None, "batch"),
        P("batch", None),
    )
    out_specs = (
        P("batch", None),
        P("batch", None),
        P("batch", "tensor"),
        P("batch", "tensor"),
        P("batch", "tensor"),
        P("tensor", "batch"),
        P("batch", "tensor"),
        P("tensor", "batch"),
        P(None, "batch"),
        P(None, "batch"),
    )
    return jax.shard_map(
        per_device, mesh=mesh, in_specs=in_specs, out_specs=out_specs, check_vma=False
    )
```

profile of v0, /device:TPU:0, one launch (start us, length us, event | category | flops | bytes accessed | tf_op | source)
XLA Modules:
  0.0 746.9 jit_solution(5650384383720290563)
XLA Ops:
  9.3 22.3 %all-gather = bf16[8,96,2]{1,2,0:T(2,128)(2,1)S(1)} all-gather(bf16[1,96,2]{1,2,0:T(2,128)(2,1)} %bitcast.189), channel_id=1, replica_groups=mesh['batch'=8,'tensor'=4] {'batch'}, dimensions={0}, use_global_device_ids=true | all-gather | bytes 3456 | tf_op jit(solution)/shard_map/all_gather | solution.py:168
  32.3 16.4 %all-gather.1 = bf16[8,96,2]{1,2,0:T(2,128)(2,1)S(1)} all-gather(bf16[1,96,2]{1,2,0:T(2,128)(2,1)} %bitcast.190), channel_id=1, replica_groups=mesh['batch'=8,'tensor'=4] {'batch'}, dimensions={0}, use_global_device_ids=true | all-gather | bytes 3456 | tf_op jit(solution)/shard_map/all_gather | solution.py:169
  54.0 31.0 %all_gather.28 = bf16[768,192]{1,0:T(8,128)(2,1)S(1)} all-gather(bf16[96,192]{1,0:T(8,128)(2,1)S(1)} %copy-done.50), channel_id=1, replica_groups=mesh['batch'=8,'tensor'=4] {'batch'}, dimensions={0}, use_global_device_ids=true | all-gather | bytes 331776 | tf_op jit(solution)/shard_map/all_gather | solution.py:163
  88.7 31.2 %all_gather.26 = bf16[768,192]{1,0:T(8,128)(2,1)S(1)} all-gather(bf16[96,192]{1,0:T(8,128)(2,1)S(1)} %copy-done.51), channel_id=1, replica_groups=mesh['batch'=8,'tensor'=4] {'batch'}, dimensions={0}, use_global_device_ids=true | all-gather | bytes 331776 | tf_op jit(solution)/shard_map/all_gather | solution.py:164
  125.1 31.3 %all_gather.29 = bf16[192,768]{0,1:T(8,128)(2,1)S(1)} all-gather(bf16[192,96]{0,1:T(8,128)(2,1)} %copy.70), channel_id=1, replica_groups=mesh['batch'=8,'tensor'=4] {'batch'}, dimensions={1}, use_global_device_ids=true | all-gather | bytes 331776 | tf_op jit(solution)/shard_map/all_gather | solution.py:165
  156.4 31.2 %all_gather.27 = bf16[768,192]{1,0:T(8,128)(2,1)S(1)} all-gather(bf16[96,192]{1,0:T(8,128)(2,1)} %param.29), channel_id=1, replica_groups=mesh['batch'=8,'tensor'=4] {'batch'}, dimensions={0}, use_global_device_ids=true | all-gather | bytes 331776 | tf_op jit(solution)/shard_map/all_gather | solution.py:162
  199.6 4.2 fusion.151
  206.3 3.2 fusion.4
  210.0 6.4 fusion.150
  222.0 90.3 %all-reduce.7.cloned.1.call-done = f32[1536,768]{1,0:T(8,128)} async-done(((f32[1536,768]{1,0:T(8,128)}), f32[1536,768]{1,0:T(8,128)}) %all-reduce.7.cloned.1.call-update) | async-done | bytes 4718608 | tf_op jit(solution)/shard_map/psum | solution.py:199
  319.5 6.2 fusion.203
  325.7 7.0 fusion.31
  334.2 4.2 fusion.204
  341.1 6.8 fusion.107
  347.9 5.9 all-to-all-start.5
  353.8 5.6 convolution_convert_fusion.5
  359.4 6.8 convolution_convert_fusion
  366.1 66.6 %all-reduce.9.cloned.1.call-done = f32[1536,768]{1,0:T(8,128)} async-done(((f32[1536,768]{1,0:T(8,128)}), f32[1536,768]{1,0:T(8,128)}) %all-reduce.9.cloned.1.call-update) | async-done | bytes 4718608 | tf_op jit(solution)/shard_map/psum | solution.py:214
  432.7 5.6 multiply_reduce_fusion.2
  438.6 4.3 multiply_add_fusion
  450.4 9.7 %fusion.128 = f32[512,3,64]{0,2,1:T(8,128)} fusion(bf16[512,3,64]{0,2,1:T(8,128)(2,1)} %bitcast.178, f32[3,512,512]{1,2,0:T(8,128)} %fusion.205, f32[3,512,512]{1,2,0:T(8,128)} %copy-done.18, f32[3,512]{1,0:T(4,128)S(1)} %copy-done.61, pred[512,512]{0,1:T(8,128)(4,1)} %copy-done.28), kind=kOutput, calls=%fused_computation.130 | convolution fusion | flops 114821120 | bytes 7149568 | tf_op jit(solution)/shard_map/while/body/eval_jaxpr/hqk,qhd->khd/dot_general | solution.py:132
  460.1 4.8 fusion.206
  465.0 5.1 fusion.207
  470.0 20.1 %fusion.145 = bf16[3,64,512]{2,1,0:T(8,128)(2,1)} fusion(bf16[1024,3,64]{0,2,1:T(8,128)(2,1)} %bitcast.171, f32[3,512,1024]{2,1,0:T(8,128)} %fusion.206, f32[3,512,1024]{2,1,0:T(8,128)} %copy-done.7, f32[3,512]{1,0:T(4,128)} %log_add_fusion.1, pred[512,1024]{1,0:T(8,128)(4,1)} %copy-done.23), kind=kOutput, calls=%fused_computation.139 | convolution fusion | flops 229739008 | bytes 13703168 | tf_op jit(solution)/shard_map/while/body/eval_jaxpr/hqk,khd->qhd/dot_general | solution.py:127
  493.5 9.8 %fusion.141 = bf16[3,64,512]{2,1,0:T(8,128)(2,1)} fusion(bf16[512,3,64]{0,2,1:T(8,128)(2,1)} %bitcast.179, f32[3,512,512]{1,2,0:T(8,128)} %fusion.205, f32[3,512,512]{1,2,0:T(8,128)} %copy-done.18, f32[3,512]{1,0:T(4,128)S(1)} %copy-done.61, pred[512,512]{0,1:T(8,128)(4,1)} %copy-done.28), kind=kOutput, calls=%fused_computation.137 | convolution fusion | flops 114919424 | bytes 6952960 | tf_op jit(solution)/shard_map/while/body/eval_jaxpr/hqk,khd->qhd/dot_general | solution.py:127
  503.3 26.8 %fusion.138 = bf16[3,64,512]{2,1,0:T(8,128)(2,1)} fusion(bf16[1536,3,64]{0,2,1:T(8,128)(2,1)S(1)} %bitcast.154, f32[3,512,1536]{2,1,0:T(8,128)} %fusion.207, f32[3,512,1536]{2,1,0:T(8,128)} %copy-done.6, f32[3,512]{1,0:T(4,128)S(1)} %copy-done.62, pred[512,1536]{1,0:T(8,128)(4,1)} %copy-done.16), kind=kOutput, calls=%fused_computation.136 | convolution fusion | flops 344558592 | bytes 20453376 | tf_op jit(solution)/shard_map/while/body/eval_jaxpr/hqk,khd->qhd/dot_general | solution.py:127
  530.0 20.4 %fusion.119 = f32[1536,3,64]{0,2,1:T(8,128)} fusion(f32[1536,3,64]{0,2,1:T(8,128)} %scatter-add.14, bf16[512,3,64]{0,2,1:T(8,128)(2,1)} %bitcast.176, f32[3,512,1024]{2,1,0:T(8,128)} %fusion.206, f32[3,512,1024]{2,1,0:T(8,128)} %copy-done.7, f32[3,512]{1,0:T(4,128)S(1)} %copy-done.63, pred[512,1024]{1,0:T(8,128)(4,1)} %copy-done.23), kind=kOutput, calls=%fused_computation.123 | convolution fusion | flops 229837312 | bytes 28000256 | tf_op jit(solution)/shard_map/while/body/eval_jaxpr/hqk,qhd->khd/dot_general | solution.py:132
  550.5 27.8 %fusion.76 = bf16[1536,3,64]{0,2,1:T(8,128)(2,1)} fusion(f32[1536,3,64]{0,2,1:T(8,128)} %fusion.119, bf16[512,3,64]{0,2,1:T(8,128)(2,1)S(1)} %bitcast.174, f32[3,512,1536]{2,1,0:T(8,128)} %fusion.207, f32[3,512,1536]{2,1,0:T(8,128)} %copy-done.6, f32[3,512]{1,0:T(4,128)S(1)} %copy-done.62, pred[512,1536]{1,0:T(8,128)(4,1)} %copy-done.16), kind=kOutput, calls=%fused_computation.94 | convolution fusion | flops 345050112 | bytes 21633024 | tf_op jit(solution)/shard_map/while/body/eval_jaxpr/hqk,qhd->khd/dot_general | solution.py:132
  578.2 4.1 fusion.208
  582.4 7.9 %fusion.125 = f32[1536,3,64]{0,2,1:T(8,128)} fusion(f32[1536,3,64]{0,2,1:T(8,128)} %scatter-add.16, bf16[512,3,64]{0,2,1:T(8,128)(2,1)S(1)} %bitcast.166, f32[3,512]{1,0:T(4,128)S(1)} %copy-done.63, pred[512,1024]{1,0:T(8,128)(4,1)S(1)} %copy-done.24, f32[3,512,1024]{2,1,0:T(8,128)} %copy-done.7), kind=kOutput, calls=%fused_computation.125 | convolution fusion | flops 212533248 | bytes 8591360 | tf_op jit(solution)/shard_map/while/body/eval_jaxpr/hqk,qhd->khd/dot_general | solution.py:140
  590.3 5.5 all-to-all-start.4
  598.2 8.8 %fusion.73 = bf16[1536,3,64]{0,2,1:T(8,128)(2,1)S(1)} fusion(f32[1536,3,64]{0,2,1:T(8,128)} %fusion.125, bf16[512,3,64]{0,2,1:T(8,128)(2,1)S(1)} %bitcast.160, f32[3,512]{1,0:T(4,128)S(1)} %copy-done.62, f32[3,512,1536]{2,1,0:T(8,128)} %copy-done.6, pred[512,1536]{1,0:T(8,128)(4,1)S(1)} %copy-done.17), kind=kOutput, calls=%fused_computation.93 | convolution fusion | flops 319094784 | bytes 12195840 | tf_op jit(solution)/shard_map/while/body/eval_jaxpr/hqk,qhd->khd/dot_general | solution.py:140
  616.4 7.8 %all-to-all-done.4 = bf16[8,96,768]{2,1,0:T(8,128)(2,1)} async-done(((bf16[8,96,768]{2,1,0:T(8,128)(2,1)}), bf16[8,96,768]{2,1,0:T(8,128)(2,1)}, u32[]{:S(2)}, u32[]{:S(2)}) %all-to-all-start.4) | async-done | bytes 1179680 | tf_op jit(solution)/shard_map/all_to_all | solution.py:18
  624.3 3.6 all-to-all-start.2
  627.9 3.4 convolution_convert_fusion.8
  635.2 4.5 all-to-all-done.2
  639.7 4.1 all-to-all-start
  644.4 3.2 convolution_convert_fusion.7
  651.6 3.7 all-to-all-done
  655.3 4.1 all-to-all-start.1
  661.6 3.9 convolution_convert_fusion.9
  670.1 3.7 all-to-all-start.3
  685.7 19.5 %all-reduce.11.cloned.1.call-done = (bf16[1536,768]{1,0:T(8,128)(2,1)}, bf16[1536,768]{1,0:T(8,128)(2,1)}) async-done(((bf16[1536,768]{1,0:T(8,128)(2,1)}, bf16[1536,768]{1,0:T(8,128)(2,1)}), (bf16[1536,768]{1,0:T(8,128)(2,1)}, bf16[1536,768]{1,0:T(8,128)(2,1)})) %all-reduce.11.cloned.1.call-update) | async-done | bytes 4718608 | tf_op jit(solution)/shard_map/psum | solution.py:206
  705.2 3.8 fusion.24
  711.7 5.5 all-to-all-start.7
  717.4 5.2 multiply_convert_fusion.4
  726.3 6.0 all-to-all-start.6
  732.9 5.9 all-to-all-done.6
  (251 shorter events, 104.7 us)
Async XLA Ops:
  8.0 77.0 %copy-start.1 = (bf16[1536,768]{1,0:T(8,128)(2,1)S(1)}, bf16[1536,768]{1,0:T(8,128)(2,1)}, u32[]{:S(2)}) copy-start(bf16[1536,768]{1,0:T(8,128)(2,1)} %param.27) | copy-start | bytes 7077892
  8.0 45.9 %copy-start.50 = (bf16[96,192]{1,0:T(8,128)(2,1)S(1)}, bf16[96,192]{1,0:T(8,128)(2,1)}, u32[]{:S(2)}) copy-start(bf16[96,192]{1,0:T(8,128)(2,1)} %param.30) | copy-start | bytes 110596
  8.0 304.2 %all-reduce.7.cloned.1.call-start = ((), (), s32[]{:S(2)}) async-start(), calls=%async_computation.8 | async-start | bytes 9437184 | tf_op jit(solution)/shard_map/psum | solution.py:199
  32.3 53.9 %copy-start.46 = (f32[768]{0:T(1024)}, f32[768]{0:T(1024)S(1)}, u32[]{:S(2)}) copy-start(f32[768]{0:T(1024)S(1)} %get-tuple-element.217) | copy-start | bytes 9220
  51.4 35.7 %copy-start.37 = (f32[1536]{0:T(1024)}, f32[1536]{0:T(1024)S(1)}, u32[]{:S(2)}) copy-start(f32[1536]{0:T(1024)S(1)} %broadcast_multiply_fusion.5) | copy-start | bytes 18436
  53.9 31.0 %copy-start.44 = (f32[1536]{0:T(1024)}, f32[1536]{0:T(1024)S(1)}, u32[]{:S(2)}) copy-start(f32[1536]{0:T(1024)S(1)} %add_rsqrt_fusion.1) | copy-start | bytes 18436
  86.2 36.1 %copy-start.3 = (bf16[1536,768]{1,0:T(8,128)(2,1)}, bf16[1536,768]{1,0:T(8,128)(2,1)S(1)}, u32[]{:S(2)}) copy-start(bf16[1536,768]{1,0:T(8,128)(2,1)S(1)} %fusion.17) | copy-start | bytes 7077892
  87.1 116.7 %copy-start.21 = (bf16[1536,192]{0,1:T(8,128)(2,1)}, bf16[1536,192]{0,1:T(8,128)(2,1)S(1)}, u32[]{:S(2)}) copy-start(bf16[1536,192]{0,1:T(8,128)(2,1)S(1)} %convolution_convert_fusion.2) | copy-start | bytes 1769476
  125.1 66.2 %copy-start.43 = (bf16[512,192]{0,1:T(8,128)(2,1)S(1)}, bf16[512,192]{0,1:T(8,128)(2,1)}, u32[]{:S(2)}) copy-start(bf16[512,192]{0,1:T(8,128)(2,1)} %slice.337) | copy-start | bytes 589828
  156.4 60.1 %copy-start.14 = (bf16[192,768]{0,1:T(8,128)(2,1)}, bf16[192,768]{0,1:T(8,128)(2,1)S(1)}, u32[]{:S(2)}) copy-start(bf16[192,768]{0,1:T(8,128)(2,1)S(1)} %all_gather.29) | copy-start | bytes 884740
  190.4 13.4 %copy-start.39 = (bf16[512,192]{0,1:T(8,128)(2,1)}, bf16[512,192]{0,1:T(8,128)(2,1)S(1)}, u32[]{:S(2)}) copy-start(bf16[512,192]{0,1:T(8,128)(2,1)S(1)} %get-tuple-element.228) | copy-start | bytes 589828
  191.2 18.3 %copy-start.16 = (pred[512,1536]{1,0:T(8,128)(4,1)}, pred[512,1536]{1,0:T(8,128)(4,1)S(1)}, u32[]{:S(2)}) copy-start(pred[512,1536]{1,0:T(8,128)(4,1)S(1)} %fusion.50) | copy-start | bytes 2359300
  197.4 6.4 copy-start.7
  197.4 6.4 copy-start.52
  209.6 6.9 copy-start.55
  219.5 100.0 %all-gather.5.cloned.1.call-start = ((), (), s32[]{:S(2)}) async-start(), calls=%async_computation.9 | async-start | bytes 1327104 | tf_op jit(solution)/shard_map/all_gather | solution.py:166
  220.1 105.6 %all-gather.7.cloned.1.call-start = ((), (), s32[]{:S(2)}) async-start(), calls=%async_computation.10 | async-start | bytes 1327104 | tf_op jit(solution)/shard_map/all_gather | solution.py:167
  220.7 212.0 %all-reduce.9.cloned.1.call-start = ((), (), s32[]{:S(2)}) async-start(), calls=%async_computation.11 | async-start | bytes 9437184 | tf_op jit(solution)/shard_map/psum | solution.py:214
  325.7 8.5 %copy-start.66 = (bf16[768,768]{1,0:T(8,128)(2,1)S(1)}, bf16[768,768]{1,0:T(8,128)(2,1)}, u32[]{:S(2)}) copy-start(bf16[768,768]{1,0:T(8,128)(2,1)} %all-gather.5.cloned.1.call-done) | copy-start | bytes 3538948
  347.9 242.4 %all-to-all-start.5 = ((bf16[8,768,96]{1,2,0:T(8,128)(2,1)}), bf16[8,768,96]{1,2,0:T(8,128)(2,1)}, u32[]{:S(2)}, u32[]{:S(2)}) async-start(bf16[8,768,96]{1,2,0:T(8,128)(2,1)} %bitcast.158), calls=%async_computation.5 | async-start | bytes 2359296 | tf_op jit(solution)/shard_map/all_to_all | solution.py:18
  353.8 5.6 copy-start.65
  432.7 5.6 copy-start.5
  432.7 5.9 copy-start.20
  432.7 5.9 copy-start.49
  432.7 5.9 copy-start.58
  470.0 22.3 %copy-start.36 = (f32[512,3,64]{0,2,1:T(8,128)S(1)}, f32[512,3,64]{0,2,1:T(8,128)}, u32[]{:S(2)}) copy-start(f32[512,3,64]{0,2,1:T(8,128)} %fusion.128) | copy-start | bytes 1179652
  493.5 9.8 %copy-start.22 = (bf16[1536,192]{0,1:T(8,128)(2,1)S(1)}, bf16[1536,192]{0,1:T(8,128)(2,1)}, u32[]{:S(2)}) copy-start(bf16[1536,192]{0,1:T(8,128)(2,1)} %copy-done.21) | copy-start | bytes 1769476
  493.5 9.8 %copy-start.62 = (f32[3,512]{1,0:T(4,128)S(1)}, f32[3,512]{1,0:T(4,128)}, u32[]{:S(2)}) copy-start(f32[3,512]{1,0:T(4,128)} %log_add_fusion) | copy-start | bytes 18436
  503.2 26.8 %copy-start.63 = (f32[3,512]{1,0:T(4,128)S(1)}, f32[3,512]{1,0:T(4,128)}, u32[]{:S(2)}) copy-start(f32[3,512]{1,0:T(4,128)} %log_add_fusion.1) | copy-start | bytes 18436
  530.0 20.4 %copy-start.40 = (bf16[512,192]{0,1:T(8,128)(2,1)S(1)}, bf16[512,192]{0,1:T(8,128)(2,1)}, u32[]{:S(2)}) copy-start(bf16[512,192]{0,1:T(8,128)(2,1)} %copy-done.39) | copy-start | bytes 589828
  550.5 27.8 %copy-start.13 = (bf16[768,192]{1,0:T(8,128)(2,1)S(1)}, bf16[768,192]{1,0:T(8,128)(2,1)}, u32[]{:S(2)}) copy-start(bf16[768,192]{1,0:T(8,128)(2,1)} %copy-done.12) | copy-start | bytes 884740
  582.4 13.7 %copy-start.11 = (bf16[768,192]{1,0:T(8,128)(2,1)S(1)}, bf16[768,192]{1,0:T(8,128)(2,1)}, u32[]{:S(2)}) copy-start(bf16[768,192]{1,0:T(8,128)(2,1)} %copy-done.10) | copy-start | bytes 884740
  590.3 34.0 %all-to-all-start.4 = ((bf16[8,96,768]{2,1,0:T(8,128)(2,1)}), bf16[8,96,768]{2,1,0:T(8,128)(2,1)}, u32[]{:S(2)}, u32[]{:S(2)}) async-start(bf16[8,96,768]{2,1,0:T(8,128)(2,1)} %bitcast.157), calls=%async_computation.4 | async-start | bytes 2359296 | tf_op jit(solution)/shard_map/all_to_all | solution.py:18
  595.8 109.4 %all-reduce.11.cloned.1.call-start = ((), (), s32[]{:S(2)}) async-start(), calls=%async_computation.12 | async-start | bytes 9437184 | tf_op jit(solution)/shard_map/psum | solution.py:206
  596.1 11.8 %slice-start.2 = ((s8[4718592]{0:T(1024)(128)(4,1)}), s8[4194304]{0:T(1024)(128)(4,1)S(1)}, s32[]{:S(2)}) async-start(s8[4718592]{0:T(1024)(128)(4,1)} %bitcast.147), calls=%async_computation.15 | async-start | bytes 8388608
  598.2 9.6 %slice-start.3 = ((s8[4718592]{0:T(1024)(128)(4,1)}), s8[524288]{0:T(1024)(128)(4,1)S(1)}, s32[]{:S(2)}) async-start(s8[4718592]{0:T(1024)(128)(4,1)} %bitcast.147), calls=%async_computation.16 | async-start | bytes 1048576
  598.2 9.6 %copy-start.9 = (bf16[768,192]{1,0:T(8,128)(2,1)S(1)}, bf16[768,192]{1,0:T(8,128)(2,1)}, u32[]{:S(2)}) copy-start(bf16[768,192]{1,0:T(8,128)(2,1)} %copy-done.8) | copy-start | bytes 884740
  624.3 15.5 %all-to-all-start.2 = ((bf16[8,96,192]{1,2,0:T(8,128)(2,1)}), bf16[8,96,192]{1,2,0:T(8,128)(2,1)S(1)}, u32[]{:S(2)}, u32[]{:S(2)}) async-start(bf16[8,96,192]{1,2,0:T(8,128)(2,1)} %copy.78), calls=%async_computation.2 | async-start | bytes 786432 | tf_op jit(solution)/shard_map/all_to_all | solution.py:18
  639.7 15.6 %all-to-all-start = ((bf16[8,96,192]{1,2,0:T(8,128)(2,1)}), bf16[8,96,192]{1,2,0:T(8,128)(2,1)}, u32[]{:S(2)}, u32[]{:S(2)}) async-start(bf16[8,96,192]{1,2,0:T(8,128)(2,1)} %copy.74), calls=%async_computation | async-start | bytes 786432 | tf_op jit(solution)/shard_map/all_to_all | solution.py:18
  655.3 14.8 %all-to-all-start.1 = ((bf16[8,96,192]{1,2,0:T(8,128)(2,1)}), bf16[8,96,192]{1,2,0:T(8,128)(2,1)}, u32[]{:S(2)}, u32[]{:S(2)}) async-start(bf16[8,96,192]{1,2,0:T(8,128)(2,1)} %copy.76), calls=%async_computation.1 | async-start | bytes 786432 | tf_op jit(solution)/shard_map/all_to_all | solution.py:18
  661.6 43.6 %copy-start.38 = (f32[1536]{0:T(1024)S(1)}, f32[1536]{0:T(1024)}, u32[]{:S(2)}) copy-start(f32[1536]{0:T(1024)} %copy-done.37) | copy-start | bytes 18436
  661.6 43.6 %copy-start.45 = (f32[1536]{0:T(1024)S(1)}, f32[1536]{0:T(1024)}, u32[]{:S(2)}) copy-start(f32[1536]{0:T(1024)} %copy-done.44) | copy-start | bytes 18436
  665.5 39.7 %copy-start.47 = (f32[768]{0:T(1024)S(1)}, f32[768]{0:T(1024)}, u32[]{:S(2)}) copy-start(f32[768]{0:T(1024)} %copy-done.46) | copy-start | bytes 9220
  670.1 14.8 %all-to-all-start.3 = ((bf16[8,192,96]{2,1,0:T(8,128)(2,1)}), bf16[8,192,96]{2,1,0:T(8,128)(2,1)S(1)}, u32[]{:S(2)}, u32[]{:S(2)}) async-start(bf16[8,192,96]{2,1,0:T(8,128)(2,1)} %bitcast.139), calls=%async_computation.3 | async-start | bytes 786432 | tf_op jit(solution)/shard_map/all_to_all | solution.py:18
  677.7 39.7 %copy-start.56 = (f32[1536]{0:T(1024)S(1)}, f32[1536]{0:T(1024)}, u32[]{:S(2)}) copy-start(f32[1536]{0:T(1024)} %fusion.154) | copy-start | bytes 18436
  705.2 17.4 %slice-start = ((s8[4718592]{0:T(1024)(128)(4,1)}), s8[524288]{0:T(1024)(128)(4,1)S(1)}, s32[]{:S(2)}) async-start(s8[4718592]{0:T(1024)(128)(4,1)} %bitcast.145), calls=%async_computation.13 | async-start | bytes 1048576
  711.7 14.6 %all-to-all-start.7 = ((bf16[8,2,96]{2,1,0:T(2,128)(2,1)}), bf16[8,2,96]{2,1,0:T(2,128)(2,1)S(1)}, u32[]{:S(2)}, u32[]{:S(2)}) async-start(bf16[8,2,96]{2,1,0:T(2,128)(2,1)} %copy.82), calls=%async_computation.7 | async-start | bytes 8192 | tf_op jit(solution)/shard_map/all_to_all | solution.py:18
  726.3 12.5 %all-to-all-start.6 = ((bf16[8,2,96]{2,1,0:T(2,128)(2,1)}), bf16[8,2,96]{2,1,0:T(2,128)(2,1)S(1)}, u32[]{:S(2)}, u32[]{:S(2)}) async-start(bf16[8,2,96]{2,1,0:T(2,128)(2,1)} %copy.81), calls=%async_computation.6 | async-start | bytes 8192 | tf_op jit(solution)/shard_map/all_to_all | solution.py:18
  (37 other events, 120.4 us)
Sparse Core Ops, SparseCore 0:
  219.7 92.5 all-reduce.6
  338.5 94.1 all-reduce.8
  610.3 94.8 all-reduce.10
Sparse Core Ops, SparseCore 1:
  222.2 39.9 all-gather.4
  264.2 40.0 all-gather.6
where the time goes:
time: 757 us; the launch traced here: 747 us
  matrix products  231 us (31%)
  waiting for transfers between devices  205 us (27%)
  blocking collectives  163 us (22%)
  other arithmetic  57.6 us (8%)
  starting transfers between devices  38.8 us (5%)
  local copies, waits for them, and re-layouts  34.2 us (5%)
  between operations  17.1 us (2%)
    psum x1, waiting for transfers between devices, per_device(): hidden = inputs + lax.psum(attn_partial, 'tensor')  90.3 us
    psum x1, waiting for transfers between devices, per_device(): grad_normed_two = lax.psum(mid_partial, 'tensor')  66.6 us
    dot_general x3, matrix products, attend_back(): jnp.einsum('hqk,qhd->khd', grad_raw, queries[begin_row:end_row], preferre...  57.9 us
    dot_general x3, matrix products, attend_back(): jnp.einsum('hqk,khd->qhd', grad_raw, key_rows[:end_row], preferred_elemen...  56.7 us
    all_to_all x8, starting transfers between devices, summed_on_arrival(): lax.all_to_all(cut_along(value, dim, length), axis, 0, 0, tiled=True)  38.4 us
    all_gather x1, blocking collectives, per_device(): lax.all_gather(w_out, 'batch', axis=1, tiled=True)  31.3 us
    all_gather x1, blocking collectives, per_device(): lax.all_gather(w_value, 'batch', axis=0, tiled=True)  31.2 us
    all_gather x1, blocking collectives, per_device(): lax.all_gather(w_query, 'batch', axis=0, tiled=True)  31.2 us
  transfers between devices with their start and end apart: 13, of which 9 were waited for; matrix products, arithmetic and copies ran while one was open for 34% of the time, Pallas kernels for 0%

commit v1 on v0

--- a/solution.py
+++ b/solution.py
@@ -2,9 +2,35 @@
 import jax.numpy as jnp
 from jax import lax
 from jax.sharding import PartitionSpec as P
+from jax.lax import axis_index, axis_size, ppermute
 
 HD = 64
 epsilon = 1e-05
+
+
+def finish_loads(sheet, out_dim):
+    then = list(sheet.shape[1:])
+    then[out_dim] *= sheet.shape[0]
+    return jnp.moveaxis(sheet, 0, out_dim).reshape(then)
+
+
+def divide_series(my_data, axis_id, dim_i):
+    num_devices = axis_size(axis_id)
+    made = list(map(lambda ii: (ii, (ii + 1) % num_devices), range(num_devices)))
+    copies = [(j0, hop_no) for hop_no, j0 in made]
+    main, z1 = ([], [])
+    for s in range(num_devices - 1):
+        if s % 2 == 0:
+            main.append(ppermute(main[-1] if main else my_data, axis_id, made))
+        else:
+            newest = ppermute(z1[-1] if z1 else my_data, axis_id, copies)
+            z1.append(newest)
+    last = jnp.stack([*main[::-1], my_data, *z1], 0)
+    back = axis_index(axis_id)
+    oldest = len(main)
+    after = back - oldest
+    last = last[(jnp.arange(num_devices) - after) % num_devices]
+    return finish_loads(last, dim_i)
 
 
 def cut_along(value, dim, length):
@@ -159,7 +185,7 @@
     block_rows = min(512, seq_len)
     scaling = float(HD) ** (-0.5)
     gathered = (
-        lax.all_gather(w_query, "batch", axis=0, tiled=True),
+        divide_series(w_query, "batch", 0),
         lax.all_gather(w_key, "batch", axis=0, tiled=True),
         lax.all_gather(w_value, "batch", axis=0, tiled=True),
         lax.all_gather(w_out, "batch", axis=1, tiled=True),

time: 757 us -> 742 us (0.980)
  blocking collectives: 163 us -> 130 us
  starting transfers between devices: 38.8 us -> 56.8 us
  local copies, waits for them, and re-layouts: 34.2 us -> 45.2 us
  matrix products: 231 us -> 222 us
    all_gather x1 -> x0, blocking collectives: 31.2 us -> none  [per_device(): lax.all_gather(w_query, 'batch', axis=0, tiled=True)]
    ppermute x0 -> x7, starting transfers between devices: none -> 15.8 us  [the longest x3 10.9 us: divide_series(): newest = ppermute(z1[-1] if z1 else my_data, axis_id, copies)]
    all_to_all x8, waiting for transfers between devices: 27.2 us -> 18 us  [summed_on_arrival(): lax.all_to_all(cut_along(value, dim, length), axis, 0, 0, tiled=True)]
    unnamed x148 -> x155, local copies, waits for them, and re-layouts: 10.3 us -> 18.2 us
  transfers between devices with their start and end apart: 13 -> 20, of which waited for: 9 -> 9; matrix products, arithmetic and copies ran while one was open for 34% -> 37% of each run, Pallas kernels for 0% -> 0%
where the time goes in v1:
time: 742 us; the launch traced here: 735 us
  matrix products  222 us (30%)
  waiting for transfers between devices  203 us (27%)
  blocking collectives  130 us (18%)
  other arithmetic  60.2 us (8%)
  starting transfers between devices  56.8 us (8%)
  local copies, waits for them, and re-layouts  45.2 us (6%)
  between operations  17.2 us (2%)
    psum x1, waiting for transfers between devices, per_device(): hidden = inputs + lax.psum(attn_partial, 'tensor')  89.1 us
    psum x1, waiting for transfers between devices, per_device(): grad_normed_two = lax.psum(mid_partial, 'tensor')  66.8 us
    dot_general x3, matrix products, attend_back(): jnp.einsum('hqk,qhd->khd', grad_raw, queries[begin_row:end_row], preferre...  54.3 us
    dot_general x3, matrix products, attend_back(): jnp.einsum('hqk,khd->qhd', grad_raw, key_rows[:end_row], preferred_elemen...  52.7 us
    all_to_all x8, starting transfers between devices, summed_on_arrival(): lax.all_to_all(cut_along(value, dim, length), axis, 0, 0, tiled=True)  40.8 us
    all_gather x1, blocking collectives, per_device(): lax.all_gather(w_out, 'batch', axis=1, tiled=True)  33.3 us
    all_gather x1, blocking collectives, per_device(): lax.all_gather(w_value, 'batch', axis=0, tiled=True)  31.1 us
    all_gather x1, blocking collectives, per_device(): lax.all_gather(w_key, 'batch', axis=0, tiled=True)  31 us
  transfers between devices with their start and end apart: 20, of which 9 were waited for; matrix products, arithmetic and copies ran while one was open for 37% of the time, Pallas kernels for 0%

profile of v1, /device:TPU:0, one launch (start us, length us, event | category | flops | bytes accessed | tf_op | source)
XLA Modules:
  0.0 735.1 jit_solution(12993207171623276223)
XLA Ops:
  8.1 3.0 collective-permute-start
  11.1 3.1 collective-permute-start.4
  16.5 18.3 %all-gather = bf16[8,96,2]{1,2,0:T(2,128)(2,1)S(1)} all-gather(bf16[1,96,2]{1,2,0:T(2,128)(2,1)} %bitcast.208), channel_id=1, replica_groups=mesh['batch'=8,'tensor'=4] {'batch'}, dimensions={0}, use_global_device_ids=true | all-gather | bytes 3456 | tf_op jit(solution)/shard_map/all_gather | solution.py:194
  35.5 16.4 %all-gather.1 = bf16[8,96,2]{1,2,0:T(2,128)(2,1)S(1)} all-gather(bf16[1,96,2]{1,2,0:T(2,128)(2,1)} %bitcast.209), channel_id=1, replica_groups=mesh['batch'=8,'tensor'=4] {'batch'}, dimensions={0}, use_global_device_ids=true | all-gather | bytes 3456 | tf_op jit(solution)/shard_map/all_gather | solution.py:195
  57.2 31.0 %all_gather.24 = bf16[768,192]{1,0:T(8,128)(2,1)S(1)} all-gather(bf16[96,192]{1,0:T(8,128)(2,1)S(1)} %copy-done.52), channel_id=1, replica_groups=mesh['batch'=8,'tensor'=4] {'batch'}, dimensions={0}, use_global_device_ids=true | all-gather | bytes 331776 | tf_op jit(solution)/shard_map/all_gather | solution.py:189
  88.1 31.1 %all_gather.23 = bf16[768,192]{1,0:T(8,128)(2,1)S(1)} all-gather(bf16[96,192]{1,0:T(8,128)(2,1)S(1)} %copy-done.53), channel_id=1, replica_groups=mesh['batch'=8,'tensor'=4] {'batch'}, dimensions={0}, use_global_device_ids=true | all-gather | bytes 331776 | tf_op jit(solution)/shard_map/all_gather | solution.py:190
  127.9 33.3 %all_gather.25 = bf16[192,768]{0,1:T(8,128)(2,1)} all-gather(bf16[192,96]{0,1:T(8,128)(2,1)} %copy.70), channel_id=1, replica_groups=mesh['batch'=8,'tensor'=4] {'batch'}, dimensions={1}, use_global_device_ids=true | all-gather | bytes 331776 | tf_op jit(solution)/shard_map/all_gather | solution.py:191
  171.3 4.9 collective-permute-start.6
  198.3 4.2 fusion.151
  205.2 3.2 fusion.4
  208.8 6.4 fusion.150
  220.8 89.1 %all-reduce.7.cloned.1.call-done = f32[1536,768]{1,0:T(8,128)} async-done(((f32[1536,768]{1,0:T(8,128)}), f32[1536,768]{1,0:T(8,128)}) %all-reduce.7.cloned.1.call-update) | async-done | bytes 4718608 | tf_op jit(solution)/shard_map/psum | solution.py:225
  317.4 6.2 fusion.204
  323.6 7.0 fusion.31
  332.1 4.2 fusion.205
  339.0 6.8 fusion.107
  345.8 5.7 all-to-all-start.5
  351.5 5.6 convolution_convert_fusion.5
  357.1 6.8 convolution_convert_fusion
  363.9 66.8 %all-reduce.9.cloned.1.call-done = f32[1536,768]{1,0:T(8,128)} async-done(((f32[1536,768]{1,0:T(8,128)}), f32[1536,768]{1,0:T(8,128)}) %all-reduce.9.cloned.1.call-update) | async-done | bytes 4718608 | tf_op jit(solution)/shard_map/psum | solution.py:240
  430.7 5.6 multiply_reduce_fusion.2
  436.5 4.4 multiply_add_fusion
  448.4 9.8 %fusion.128 = f32[512,3,64]{0,2,1:T(8,128)} fusion(bf16[512,3,64]{0,2,1:T(8,128)(2,1)} %bitcast.197, f32[3,512,512]{1,2,0:T(8,128)} %fusion.206, f32[3,512,512]{1,2,0:T(8,128)} %copy-done.18, f32[3,512]{1,0:T(4,128)S(1)} %copy-done.62, pred[512,512]{0,1:T(8,128)(4,1)} %compare_and_fusion.1), kind=kOutput, calls=%fused_computation.131 | convolution fusion | flops 114821120 | bytes 7149568 | tf_op jit(solution)/shard_map/while/body/eval_jaxpr/hqk,qhd->khd/dot_general | solution.py:158
  462.4 4.8 fusion.207
  467.3 5.1 fusion.208
  472.4 26.9 %fusion.138 = bf16[3,64,512]{2,1,0:T(8,128)(2,1)} fusion(bf16[1536,3,64]{0,2,1:T(8,128)(2,1)} %bitcast.172, f32[3,512,1536]{2,1,0:T(8,128)} %fusion.208, f32[3,512,1536]{2,1,0:T(8,128)} %copy-done.6, f32[3,512]{1,0:T(4,128)S(1)} %copy-done.63, pred[512,1536]{1,0:T(8,128)(4,1)} %fusion.50), kind=kOutput, calls=%fused_computation.137 | convolution fusion | flops 344558592 | bytes 20453376 | tf_op jit(solution)/shard_map/while/body/eval_jaxpr/hqk,khd->qhd/dot_general | solution.py:153
  499.2 16.1 %fusion.145 = bf16[3,64,512]{2,1,0:T(8,128)(2,1)} fusion(bf16[1024,3,64]{0,2,1:T(8,128)(2,1)} %bitcast.190, f32[3,512,1024]{2,1,0:T(8,128)} %fusion.207, f32[3,512,1024]{2,1,0:T(8,128)} %copy-done.7, f32[3,512]{1,0:T(4,128)S(1)} %copy-done.64, pred[512,1024]{1,0:T(8,128)(4,1)S(1)} %copy-done.24), kind=kOutput, calls=%fused_computation.140 | convolution fusion | flops 229739008 | bytes 13703168 | tf_op jit(solution)/shard_map/while/body/eval_jaxpr/hqk,khd->qhd/dot_general | solution.py:153
  515.3 16.8 %fusion.119 = f32[1536,3,64]{0,2,1:T(8,128)} fusion(f32[1536,3,64]{0,2,1:T(8,128)} %scatter-add.14, bf16[512,3,64]{0,2,1:T(8,128)(2,1)} %bitcast.195, f32[3,512,1024]{2,1,0:T(8,128)} %fusion.207, f32[3,512,1024]{2,1,0:T(8,128)} %copy-done.7, f32[3,512]{1,0:T(4,128)S(1)} %copy-done.64, pred[512,1024]{1,0:T(8,128)(4,1)S(1)} %copy-done.24), kind=kOutput, calls=%fused_computation.124 | convolution fusion | flops 229837312 | bytes 28000256 | tf_op jit(solution)/shard_map/while/body/eval_jaxpr/hqk,qhd->khd/dot_general | solution.py:158
  532.2 8.0 %fusion.125 = f32[1536,3,64]{0,2,1:T(8,128)} fusion(f32[1536,3,64]{0,2,1:T(8,128)} %scatter-add.16, bf16[512,3,64]{0,2,1:T(8,128)(2,1)} %bitcast.185, f32[3,512]{1,0:T(4,128)S(1)} %copy-done.64, pred[512,1024]{1,0:T(8,128)(4,1)S(1)} %copy-done.24, f32[3,512,1024]{2,1,0:T(8,128)} %copy-done.7), kind=kOutput, calls=%fused_computation.126 | convolution fusion | flops 212533248 | bytes 8591360 | tf_op jit(solution)/shard_map/while/body/eval_jaxpr/hqk,qhd->khd/dot_general | solution.py:166
  540.2 9.7 %fusion.73 = bf16[1536,3,64]{0,2,1:T(8,128)(2,1)} fusion(f32[1536,3,64]{0,2,1:T(8,128)} %fusion.125, bf16[512,3,64]{0,2,1:T(8,128)(2,1)S(1)} %bitcast.179, f32[3,512]{1,0:T(4,128)S(1)} %copy-done.63, f32[3,512,1536]{2,1,0:T(8,128)} %copy-done.6, pred[512,1536]{1,0:T(8,128)(4,1)S(1)} %copy-done.17), kind=kOutput, calls=%fused_computation.94 | convolution fusion | flops 319094784 | bytes 12195840 | tf_op jit(solution)/shard_map/while/body/eval_jaxpr/hqk,qhd->khd/dot_general | solution.py:166
  549.9 5.5 all-to-all-start.4
  555.5 9.7 %fusion.141 = bf16[3,64,512]{2,1,0:T(8,128)(2,1)} fusion(bf16[512,3,64]{0,2,1:T(8,128)(2,1)S(1)} %bitcast.199, f32[3,512,512]{1,2,0:T(8,128)} %fusion.206, f32[3,512,512]{1,2,0:T(8,128)} %copy-done.18, f32[3,512]{1,0:T(4,128)S(1)} %copy-done.62, pred[512,512]{0,1:T(8,128)(4,1)} %compare_and_fusion.1), kind=kOutput, calls=%fused_computation.138 | convolution fusion | flops 114919424 | bytes 6952960 | tf_op jit(solution)/shard_map/while/body/eval_jaxpr/hqk,khd->qhd/dot_general | solution.py:153
  565.1 27.8 %fusion.76 = bf16[1536,3,64]{0,2,1:T(8,128)(2,1)} fusion(f32[1536,3,64]{0,2,1:T(8,128)} %fusion.119, bf16[512,3,64]{0,2,1:T(8,128)(2,1)S(1)} %bitcast.193, f32[3,512,1536]{2,1,0:T(8,128)} %fusion.208, f32[3,512,1536]{2,1,0:T(8,128)} %copy-done.6, f32[3,512]{1,0:T(4,128)S(1)} %copy-done.63, pred[512,1536]{1,0:T(8,128)(4,1)} %fusion.50), kind=kOutput, calls=%fused_computation.95 | convolution fusion | flops 345050112 | bytes 21633024 | tf_op jit(solution)/shard_map/while/body/eval_jaxpr/hqk,qhd->khd/dot_general | solution.py:158
  599.3 3.0 convolution_convert_fusion.6
  604.5 5.9 all-to-all-start.2
  610.5 3.4 convolution_convert_fusion.8
  617.9 3.6 all-to-all-done.2
  621.4 4.4 all-to-all-start
  626.4 3.3 convolution_convert_fusion.7
  636.6 4.1 all-to-all-start.1
  642.9 3.7 convolution_convert_fusion.9
  651.5 3.7 all-to-all-start.3
  667.0 26.2 %all-reduce.11.cloned.1.call-done = (bf16[1536,768]{1,0:T(8,128)(2,1)}, bf16[1536,768]{1,0:T(8,128)(2,1)}) async-done(((bf16[1536,768]{1,0:T(8,128)(2,1)}, bf16[1536,768]{1,0:T(8,128)(2,1)}), (bf16[1536,768]{1,0:T(8,128)(2,1)}, bf16[1536,768]{1,0:T(8,128)(2,1)})) %all-reduce.11.cloned.1.call-update) | async-done | bytes 4718608 | tf_op jit(solution)/shard_map/psum | solution.py:232
  693.2 3.8 fusion.24
  699.8 5.5 all-to-all-start.7
  705.4 5.2 multiply_convert_fusion.4
  714.4 6.0 all-to-all-start.6
  721.0 5.9 all-to-all-done.6
  (274 shorter events, 127.0 us)
Async XLA Ops:
  8.0 111.2 %copy-start.1 = (bf16[1536,768]{1,0:T(8,128)(2,1)S(1)}, bf16[1536,768]{1,0:T(8,128)(2,1)}, u32[]{:S(2)}) copy-start(bf16[1536,768]{1,0:T(8,128)(2,1)} %param.27) | copy-start | bytes 7077892
  8.0 49.1 %copy-start.52 = (bf16[96,192]{1,0:T(8,128)(2,1)S(1)}, bf16[96,192]{1,0:T(8,128)(2,1)}, u32[]{:S(2)}) copy-start(bf16[96,192]{1,0:T(8,128)(2,1)} %param.30) | copy-start | bytes 110596
  8.0 80.1 %copy-start.53 = (bf16[96,192]{1,0:T(8,128)(2,1)S(1)}, bf16[96,192]{1,0:T(8,128)(2,1)}, u32[]{:S(2)}) copy-start(bf16[96,192]{1,0:T(8,128)(2,1)} %param.31) | copy-start | bytes 110596
  8.0 301.9 %all-reduce.7.cloned.1.call-start = ((), (), s32[]{:S(2)}) async-start(), calls=%async_computation.8 | async-start | bytes 9437184 | tf_op jit(solution)/shard_map/psum | solution.py:225
  8.1 119.8 %collective-permute-start = (bf16[96,192]{1,0:T(8,128)(2,1)}, bf16[96,192]{1,0:T(8,128)(2,1)}, u32[]{:S(2)}, u32[]{:S(2)}) collective-permute-start(bf16[96,192]{1,0:T(8,128)(2,1)} %param.29), channel_id=1, source_target_pairs={{0,4},{4,8},{8,12},{12,16},{16,20},{20,24},{24,28},{28,0},{1,5},{5... | collective-permute-start | bytes 110600 | tf_op jit(solution)/shard_map/ppermute | solution.py:24
  11.1 152.0 %collective-permute-start.4 = (bf16[96,192]{1,0:T(8,128)(2,1)}, bf16[96,192]{1,0:T(8,128)(2,1)}, u32[]{:S(2)}, u32[]{:S(2)}) collective-permute-start(bf16[96,192]{1,0:T(8,128)(2,1)} %param.29), channel_id=1, source_target_pairs={{4,0},{8,4},{12,8},{16,12},{20,16},{24,20},{28,24},{0,28},{5,1},{9... | collective-permute-start | bytes 110600 | tf_op jit(solution)/shard_map/ppermute | solution.py:26
  35.5 84.9 %copy-start.48 = (f32[768]{0:T(1024)}, f32[768]{0:T(1024)S(1)}, u32[]{:S(2)}) copy-start(f32[768]{0:T(1024)S(1)} %get-tuple-element.217) | copy-start | bytes 9220
  54.6 66.8 %copy-start.35 = (f32[1536]{0:T(1024)}, f32[1536]{0:T(1024)S(1)}, u32[]{:S(2)}) copy-start(f32[1536]{0:T(1024)S(1)} %broadcast_multiply_fusion.5) | copy-start | bytes 18436
  57.2 62.0 %copy-start.46 = (f32[1536]{0:T(1024)}, f32[1536]{0:T(1024)S(1)}, u32[]{:S(2)}) copy-start(f32[1536]{0:T(1024)S(1)} %add_rsqrt_fusion.1) | copy-start | bytes 18436
  88.1 34.6 %copy-start.10 = (bf16[768,192]{1,0:T(8,128)(2,1)}, bf16[768,192]{1,0:T(8,128)(2,1)S(1)}, u32[]{:S(2)}) copy-start(bf16[768,192]{1,0:T(8,128)(2,1)S(1)} %all_gather.24) | copy-start | bytes 884740
  121.8 61.9 %copy-start.21 = (bf16[1536,192]{0,1:T(8,128)(2,1)}, bf16[1536,192]{0,1:T(8,128)(2,1)S(1)}, u32[]{:S(2)}) copy-start(bf16[1536,192]{0,1:T(8,128)(2,1)S(1)} %convolution_convert_fusion.2) | copy-start | bytes 1769476
  127.9 33.3 %collective-permute-start.1 = (bf16[96,192]{1,0:T(8,128)(2,1)}, bf16[96,192]{1,0:T(8,128)(2,1)}, u32[]{:S(2)}, u32[]{:S(2)}) collective-permute-start(bf16[96,192]{1,0:T(8,128)(2,1)} %collective-permute-done), channel_id=1, source_target_pairs={{0,4},{4,8},{8,12},{12,16},{16,20},{20,24},{24,28},{28,0},{1,5},{5... | collective-permute-start | bytes 110600 | tf_op jit(solution)/shard_map/ppermute | solution.py:24
  161.3 7.0 collective-permute-start.2
  163.2 8.1 %collective-permute-start.5 = (bf16[96,192]{1,0:T(8,128)(2,1)}, bf16[96,192]{1,0:T(8,128)(2,1)S(1)}, u32[]{:S(2)}, u32[]{:S(2)}) collective-permute-start(bf16[96,192]{1,0:T(8,128)(2,1)} %collective-permute-done.4), channel_id=1, source_target_pairs={{4,0},{8,4},{12,8},{16,12},{20,16},{24,20},{28,24},{0,28},{5,1},{9... | collective-permute-start | bytes 110600 | tf_op jit(solution)/shard_map/ppermute | solution.py:26
  168.3 7.9 %collective-permute-start.3 = (bf16[96,192]{1,0:T(8,128)(2,1)S(1)}, bf16[96,192]{1,0:T(8,128)(2,1)S(1)}, u32[]{:S(2)}, u32[]{:S(2)}) collective-permute-start(bf16[96,192]{1,0:T(8,128)(2,1)S(1)} %collective-permute-done.2), channel_id=1, source_target_pairs={{0,4},{4,8},{8,12},{12,16},{16,20},{20,24},{24,28},{28,0},{1,5},{5... | collective-permute-start | bytes 110600 | tf_op jit(solution)/shard_map/ppermute | solution.py:24
  171.3 12.5 %collective-permute-start.6 = (bf16[96,192]{1,0:T(8,128)(2,1)S(1)}, bf16[96,192]{1,0:T(8,128)(2,1)S(1)}, u32[]{:S(2)}, u32[]{:S(2)}) collective-permute-start(bf16[96,192]{1,0:T(8,128)(2,1)S(1)} %collective-permute-done.5), channel_id=1, source_target_pairs={{4,0},{8,4},{12,8},{16,12},{20,16},{24,20},{28,24},{0,28},{5,1},{9... | collective-permute-start | bytes 110600 | tf_op jit(solution)/shard_map/ppermute | solution.py:26
  186.0 6.2 copy-start.8
  188.8 13.8 %copy-start.37 = (bf16[512,192]{0,1:T(8,128)(2,1)}, bf16[512,192]{0,1:T(8,128)(2,1)S(1)}, u32[]{:S(2)}) copy-start(bf16[512,192]{0,1:T(8,128)(2,1)S(1)} %get-tuple-element.228) | copy-start | bytes 589828
  196.1 6.5 copy-start.7
  196.1 6.5 copy-start.54
  208.4 6.9 copy-start.57
  208.8 6.5 copy-start.14
  218.4 99.1 %all-gather.5.cloned.1.call-start = ((), (), s32[]{:S(2)}) async-start(), calls=%async_computation.9 | async-start | bytes 1327104 | tf_op jit(solution)/shard_map/all_gather | solution.py:192
  218.9 104.7 %all-gather.7.cloned.1.call-start = ((), (), s32[]{:S(2)}) async-start(), calls=%async_computation.10 | async-start | bytes 1327104 | tf_op jit(solution)/shard_map/all_gather | solution.py:193
  219.5 211.1 %all-reduce.9.cloned.1.call-start = ((), (), s32[]{:S(2)}) async-start(), calls=%async_computation.11 | async-start | bytes 9437184 | tf_op jit(solution)/shard_map/psum | solution.py:240
  323.6 8.5 %copy-start.68 = (bf16[768,768]{1,0:T(8,128)(2,1)S(1)}, bf16[768,768]{1,0:T(8,128)(2,1)}, u32[]{:S(2)}) copy-start(bf16[768,768]{1,0:T(8,128)(2,1)} %all-gather.5.cloned.1.call-done) | copy-start | bytes 3538948
  345.8 204.1 %all-to-all-start.5 = ((bf16[8,768,96]{1,2,0:T(8,128)(2,1)}), bf16[8,768,96]{1,2,0:T(8,128)(2,1)}, u32[]{:S(2)}, u32[]{:S(2)}) async-start(bf16[8,768,96]{1,2,0:T(8,128)(2,1)} %bitcast.177), calls=%async_computation.5 | async-start | bytes 2359296 | tf_op jit(solution)/shard_map/all_to_all | solution.py:44
  458.1 9.1 %copy-start.26 = (bf16[512,192]{0,1:T(8,128)(2,1)S(1)}, bf16[512,192]{0,1:T(8,128)(2,1)}, u32[]{:S(2)}) copy-start(bf16[512,192]{0,1:T(8,128)(2,1)} %get-tuple-element.224) | copy-start | bytes 589828
  472.3 26.9 %copy-start.24 = (pred[512,1024]{1,0:T(8,128)(4,1)S(1)}, pred[512,1024]{1,0:T(8,128)(4,1)}, u32[]{:S(2)}) copy-start(pred[512,1024]{1,0:T(8,128)(4,1)} %compare_and_fusion) | copy-start | bytes 1572868
  472.3 26.9 %copy-start.64 = (f32[3,512]{1,0:T(4,128)S(1)}, f32[3,512]{1,0:T(4,128)}, u32[]{:S(2)}) copy-start(f32[3,512]{1,0:T(4,128)} %log_add_fusion.1) | copy-start | bytes 18436
  532.2 8.0 %copy-start.17 = (pred[512,1536]{1,0:T(8,128)(4,1)S(1)}, pred[512,1536]{1,0:T(8,128)(4,1)}, u32[]{:S(2)}) copy-start(pred[512,1536]{1,0:T(8,128)(4,1)} %fusion.50) | copy-start | bytes 2359300
  532.2 8.0 %copy-start.27 = (bf16[512,192]{0,1:T(8,128)(2,1)S(1)}, bf16[512,192]{0,1:T(8,128)(2,1)}, u32[]{:S(2)}) copy-start(bf16[512,192]{0,1:T(8,128)(2,1)} %get-tuple-element.224) | copy-start | bytes 589828
  540.1 15.3 %copy-start.42 = (bf16[512,192]{0,1:T(8,128)(2,1)S(1)}, bf16[512,192]{0,1:T(8,128)(2,1)}, u32[]{:S(2)}) copy-start(bf16[512,192]{0,1:T(8,128)(2,1)} %slice.339) | copy-start | bytes 589828
  549.9 54.7 %all-to-all-start.4 = ((bf16[8,96,768]{2,1,0:T(8,128)(2,1)}), bf16[8,96,768]{2,1,0:T(8,128)(2,1)}, u32[]{:S(2)}, u32[]{:S(2)}) async-start(bf16[8,96,768]{2,1,0:T(8,128)(2,1)} %bitcast.176), calls=%async_computation.4 | async-start | bytes 2359296 | tf_op jit(solution)/shard_map/all_to_all | solution.py:44
  555.4 9.8 %copy-start.38 = (bf16[512,192]{0,1:T(8,128)(2,1)S(1)}, bf16[512,192]{0,1:T(8,128)(2,1)}, u32[]{:S(2)}) copy-start(bf16[512,192]{0,1:T(8,128)(2,1)} %copy-done.37) | copy-start | bytes 589828
  555.4 137.8 %all-reduce.11.cloned.1.call-start = ((), (), s32[]{:S(2)}) async-start(), calls=%async_computation.12 | async-start | bytes 9437184 | tf_op jit(solution)/shard_map/psum | solution.py:232
  565.1 27.8 %copy-start.13 = (bf16[768,192]{1,0:T(8,128)(2,1)S(1)}, bf16[768,192]{1,0:T(8,128)(2,1)}, u32[]{:S(2)}) copy-start(bf16[768,192]{1,0:T(8,128)(2,1)} %copy-done.12) | copy-start | bytes 884740
  604.5 16.9 %all-to-all-start.2 = ((bf16[8,96,192]{1,2,0:T(8,128)(2,1)}), bf16[8,96,192]{1,2,0:T(8,128)(2,1)S(1)}, u32[]{:S(2)}, u32[]{:S(2)}) async-start(bf16[8,96,192]{1,2,0:T(8,128)(2,1)} %copy.78), calls=%async_computation.2 | async-start | bytes 786432 | tf_op jit(solution)/shard_map/all_to_all | solution.py:44
  621.4 15.2 %all-to-all-start = ((bf16[8,96,192]{1,2,0:T(8,128)(2,1)}), bf16[8,96,192]{1,2,0:T(8,128)(2,1)}, u32[]{:S(2)}, u32[]{:S(2)}) async-start(bf16[8,96,192]{1,2,0:T(8,128)(2,1)} %copy.74), calls=%async_computation | async-start | bytes 786432 | tf_op jit(solution)/shard_map/all_to_all | solution.py:44
  636.6 14.9 %all-to-all-start.1 = ((bf16[8,96,192]{1,2,0:T(8,128)(2,1)}), bf16[8,96,192]{1,2,0:T(8,128)(2,1)}, u32[]{:S(2)}, u32[]{:S(2)}) async-start(bf16[8,96,192]{1,2,0:T(8,128)(2,1)} %copy.76), calls=%async_computation.1 | async-start | bytes 786432 | tf_op jit(solution)/shard_map/all_to_all | solution.py:44
  642.9 50.4 %copy-start.36 = (f32[1536]{0:T(1024)S(1)}, f32[1536]{0:T(1024)}, u32[]{:S(2)}) copy-start(f32[1536]{0:T(1024)} %copy-done.35) | copy-start | bytes 18436
  642.9 50.4 %copy-start.47 = (f32[1536]{0:T(1024)S(1)}, f32[1536]{0:T(1024)}, u32[]{:S(2)}) copy-start(f32[1536]{0:T(1024)} %copy-done.46) | copy-start | bytes 18436
  646.6 46.6 %copy-start.49 = (f32[768]{0:T(1024)S(1)}, f32[768]{0:T(1024)}, u32[]{:S(2)}) copy-start(f32[768]{0:T(1024)} %copy-done.48) | copy-start | bytes 9220
  651.5 14.8 %all-to-all-start.3 = ((bf16[8,192,96]{2,1,0:T(8,128)(2,1)}), bf16[8,192,96]{2,1,0:T(8,128)(2,1)S(1)}, u32[]{:S(2)}, u32[]{:S(2)}) async-start(bf16[8,192,96]{2,1,0:T(8,128)(2,1)} %bitcast.158), calls=%async_computation.3 | async-start | bytes 786432 | tf_op jit(solution)/shard_map/all_to_all | solution.py:44
  659.0 46.4 %copy-start.58 = (f32[1536]{0:T(1024)S(1)}, f32[1536]{0:T(1024)}, u32[]{:S(2)}) copy-start(f32[1536]{0:T(1024)} %fusion.153) | copy-start | bytes 18436
  693.2 17.4 %slice-start = ((s8[4718592]{0:T(1024)(128)(4,1)}), s8[524288]{0:T(1024)(128)(4,1)S(1)}, s32[]{:S(2)}) async-start(s8[4718592]{0:T(1024)(128)(4,1)} %bitcast.164), calls=%async_computation.13 | async-start | bytes 1048576
  699.8 14.6 %all-to-all-start.7 = ((bf16[8,2,96]{2,1,0:T(2,128)(2,1)}), bf16[8,2,96]{2,1,0:T(2,128)(2,1)S(1)}, u32[]{:S(2)}, u32[]{:S(2)}) async-start(bf16[8,2,96]{2,1,0:T(2,128)(2,1)} %copy.82), calls=%async_computation.7 | async-start | bytes 8192 | tf_op jit(solution)/shard_map/all_to_all | solution.py:44
  714.4 12.5 %all-to-all-start.6 = ((bf16[8,2,96]{2,1,0:T(2,128)(2,1)}), bf16[8,2,96]{2,1,0:T(2,128)(2,1)S(1)}, u32[]{:S(2)}, u32[]{:S(2)}) async-start(bf16[8,2,96]{2,1,0:T(2,128)(2,1)} %copy.81), calls=%async_computation.6 | async-start | bytes 8192 | tf_op jit(solution)/shard_map/all_to_all | solution.py:44
  (44 other events, 160.9 us)
Sparse Core Ops, SparseCore 0:
  218.5 91.3 all-reduce.6
  336.4 94.1 all-reduce.8
  598.4 94.7 all-reduce.10
Sparse Core Ops, SparseCore 1:
  221.0 38.7 all-gather.4
  261.9 40.0 all-gather.6
